TPU v7x, 32 devices: a whole 2x2x4 slice. The times are simulated.
32 devices in a mesh: sec: 4 (over y, core), row: 2 (over x), col: 4 (over z).
Axes of the slice: x: 2, y: 2, z: 4, core: 2. Of those that a mesh axis runs over, the one named last changes fastest.
Arguments:
- child_inv: bfloat16 [4, 4096, 4096], P('sec', 'col', 'row'), as said below
- child_low: bfloat16 [4, 2048, 4096], P('sec', 'row', 'col'), may hold values from -0.09375 to 0.09375
- parent_inv: bfloat16 [4, 6144, 3072], P('sec', 'col', 'row'), as said below
- parent_low: bfloat16 [4, 2048, 3072], P('sec', 'row', 'col'), may hold values from -0.078125 to 0.078125
- root_inv: bfloat16 [12288, 12288], P('col', ('sec', 'row')), as said below
- child_map: int32 [4, 2048], replicated, may hold values from 0 to 8191, as said below
- parent_map: int32 [2, 2048], replicated, may hold values from 0 to 12287, as said below
- child_rhs: float32 [4, 4096, 512], P('sec', 'row', 'col'), may hold values from -6 to 6
- parent_rhs: float32 [4, 3072, 512], P('sec', 'row', 'col'), may hold values from -6 to 6
- root_rhs: float32 [12288, 512], P(('sec', 'row'), 'col'), may hold values from -6 to 6
- child_back: float32 [4, 4096, 512], P('sec', 'col', 'row'), may hold values from -6 to 6
- parent_back: float32 [4, 3072, 512], P('sec', 'col', 'row'), may hold values from -6 to 6
- root_back: float32 [4, 3072, 512], P('col', ('sec', 'row')), may hold values from -6 to 6
Outputs:
- child_up: float32 [4, 4096, 512], P('sec', 'col', 'row')
- parent_up: float32 [4, 3072, 512], P('sec', 'col', 'row')
- root_up: float32 [4, 3072, 512], P('col', ('sec', 'row'))
- child_x: float32 [4, 4096, 512], P('sec', 'row', 'col')
- parent_x: float32 [4, 3072, 512], P('sec', 'row', 'col')
- root_x: float32 [12288, 512], P(('sec', 'row'), 'col')
Inputs may be any that keep to these rules, and one draw needn't show every extreme that they name: `child_inv`: zero above the diagonal of each child pivot block. `parent_inv`: the two halves side by side are zero above the diagonal. `root_inv`: zero above the diagonal. `child_map`: entries of one row are distinct; row s points into the front of parent s // 2. `parent_map`: entries of one row are distinct.
All inputs are finite; a program needn't handle non-finite values.
Results may differ from a plain program's by a relative error of at most 0.014.
Values may be sent and summed in bfloat16 or wider, within the bound.
No kernel may reach another device: no remote copies, remote signals or barrier semaphores. Data moves between devices by JAX's collectives and lax.ppermute only.
A program may use at most 128 MiB of HBM per device.

v0:
```python
import jax
import jax.numpy as jnp
from jax import lax
from jax.sharding import PartitionSpec as P

C1 = 2048
P2 = 6144
C2 = 2048
P3 = 12288


def from_partner(x, axis, bit):
    return lax.ppermute(x, axis, [(i, i ^ 1 << bit) for i in range(lax.axis_size(axis))])


def spread_cols(block):
    return lax.all_gather(block, "col", axis=1, tiled=True)


def spread_rows(block):
    return lax.all_gather(block, "row", axis=1, tiled=True)


def sum_rows(block):
    return lax.psum_scatter(block, "row", scatter_dimension=1, tiled=True)


def sum_cols(block):
    return lax.psum_scatter(block, "col", scatter_dimension=1, tiled=True)


def pair_sums(block):
    return from_partner(block, "sec", 0)


def pair_values(block):
    return from_partner(block, "sec", 0)


def root_gather(block):
    return lax.all_gather(block, ("sec", "row"), axis=0, tiled=True)


def matmul(left, right):
    return jnp.dot(left, right, preferred_element_type=jnp.float32)


def front_slot(target, n_row):
    pivot_rows = P2 // (2 * n_row)
    cont_rows = C2 // (2 * n_row)
    stride = pivot_rows + cont_rows
    half_size = P2 // 2
    pivot_slot = (
        target // half_size * n_row + target % half_size // pivot_rows
    ) * stride + target % pivot_rows
    offset = target - P2
    cont_slot = (
        (offset % (2 * cont_rows) // cont_rows * n_row + offset // (2 * cont_rows)) * stride
        + pivot_rows
        + offset % cont_rows
    )
    return jnp.where(target < P2, pivot_slot, cont_slot)


def place_rows(values, slots, first, count):
    local = slots - first
    inside = (local >= 0) & (local < count)
    target = jnp.where(inside, local, count)
    return jnp.zeros((count, values.shape[1]), jnp.float32).at[target].add(values, mode="drop")


def pair_reduce(block, pair_side):
    amount = block.shape[0] // 2
    keep = lax.dynamic_slice_in_dim(block, pair_side * amount, amount, 0)
    away = lax.dynamic_slice_in_dim(block, (1 - pair_side) * amount, amount, 0)
    return keep + pair_sums(away)


def pair_join(mine, other, pair_side):
    return jnp.where(
        pair_side == 0, jnp.concatenate([mine, other], 0), jnp.concatenate([other, mine], 0)
    )


def per_device(
    child_inv,
    child_low,
    parent_inv,
    parent_low,
    root_inv,
    child_map,
    parent_map,
    child_rhs,
    parent_rhs,
    root_rhs,
    child_back,
    parent_back,
    root_back,
):
    n_row = lax.axis_size("row")
    n_sec = lax.axis_size("sec")
    section = lax.axis_index("sec")
    row_id = lax.axis_index("row")
    pair_side = section % 2
    parent_id = section // 2
    place_id = section * n_row + row_id
    pivot_rows = P2 // (2 * n_row)
    cont_rows = C2 // (2 * n_row)
    stride = pivot_rows + cont_rows
    root_block = P3 // (n_sec * n_row)
    child_tile = child_inv[0]
    partial_value = matmul(child_tile, spread_cols(child_rhs[0].astype(jnp.bfloat16)))
    child_up = sum_rows(partial_value)
    solved = spread_rows(child_up.astype(jnp.bfloat16))
    contrib = -sum_cols(matmul(child_low[0], solved))
    own_map = lax.dynamic_slice_in_dim(child_map, section, 1, 0)[0]
    child_slots = front_slot(own_map, n_row)
    own_rows = lax.all_gather(contrib, "row", axis=0, tiled=True)
    partner_rows = pair_sums(own_rows)
    partner_map = lax.dynamic_slice_in_dim(child_map, section + 1 - 2 * pair_side, 1, 0)[0]
    first = (pair_side * n_row + row_id) * stride
    front = place_rows(own_rows, child_slots, first, stride) + place_rows(
        partner_rows, front_slot(partner_map, n_row), first, stride
    )
    pivot_in = parent_rhs[0] + front[:pivot_rows]
    share = sum_rows(matmul(parent_inv[0], spread_cols(pivot_in.astype(jnp.bfloat16))))
    parent_up = pair_reduce(share, pair_side)
    update = sum_cols(matmul(parent_low[0], spread_rows(parent_up.astype(jnp.bfloat16))))
    contrib_two = front[pivot_rows:] - pair_reduce(update, pair_side)
    map_row = lax.dynamic_slice_in_dim(parent_map, parent_id, 1, 0)[0]
    every = lax.all_gather(
        contrib_two.astype(jnp.bfloat16), ("sec", "row"), axis=0, tiled=True
    ).astype(contrib_two.dtype)
    order = parent_map.reshape(2, n_row, 2, cont_rows).transpose(0, 2, 1, 3).reshape(-1)
    root_front = place_rows(every, order, place_id * root_block, root_block)
    root_in = root_rhs + root_front
    root_wide = spread_cols(root_in.astype(jnp.bfloat16))
    root_part = matmul(root_inv, root_wide)
    root_up = lax.psum_scatter(
        root_part.astype(jnp.bfloat16), ("sec", "row"), scatter_dimension=0, tiled=True
    ).astype(jnp.float32)
    back_wide = root_gather(root_back[0].astype(jnp.bfloat16))
    root_x = sum_cols(matmul(root_inv.T, back_wide))
    root_all = root_gather(root_x.astype(jnp.bfloat16))
    block_targets = lax.dynamic_slice_in_dim(map_row, row_id * 2 * cont_rows, 2 * cont_rows)
    picked = jnp.take(root_all, block_targets, axis=0)
    residue = parent_back[0] - sum_rows(matmul(parent_low[0].T, spread_cols(picked)))
    residue_wide = spread_rows(residue.astype(jnp.bfloat16))
    full_residue = pair_join(residue_wide, pair_values(residue_wide), pair_side)
    parent_x = sum_cols(matmul(parent_inv[0].T, full_residue))
    own_cont = lax.dynamic_slice_in_dim(picked, pair_side * cont_rows, cont_rows, 0)
    front_x = jnp.concatenate([parent_x.astype(jnp.bfloat16), own_cont], 0)
    side_rows = lax.all_gather(front_x, "row", axis=0, tiled=True)
    whole_front = pair_join(side_rows, pair_values(side_rows), pair_side)
    child_count = C1 // n_row
    row_slots = lax.dynamic_slice_in_dim(child_slots, row_id * child_count, child_count)
    chosen = jnp.take(whole_front, row_slots, axis=0)
    residue_one = child_back[0] - sum_rows(matmul(child_low[0].T, spread_cols(chosen)))
    child_x = sum_cols(matmul(child_tile.T, spread_rows(residue_one.astype(jnp.bfloat16))))
    return (child_up[None], parent_up[None], root_up[None], child_x[None], parent_x[None], root_x)


def solution(mesh):
    return jax.shard_map(
        per_device,
        mesh=mesh,
        in_specs=(
            P("sec", "col", "row"),
            P("sec", "row", "col"),
            P("sec", "col", "row"),
            P("sec", "row", "col"),
            P("col", ("sec", "row")),
            P(),
            P(),
            P("sec", "row", "col"),
            P("sec", "row", "col"),
            P(("sec", "row"), "col"),
            P("sec", "col", "row"),
            P("sec", "col", "row"),
            P("col", ("sec", "row"), None),
        ),
        out_specs=(
            P("sec", "col", "row"),
            P("sec", "col", "row"),
            P("col", ("sec", "row"), None),
            P("sec", "row", "col"),
            P("sec", "row", "col"),
            P(("sec", "row"), "col"),
        ),
        check_vma=False,
    )
```

profile of v0, /device:TPU:0, one launch (start us, length us, event | category | flops | bytes accessed | tf_op | source)
XLA Modules:
  0.0 813.7 jit_solution(5113649186124741698)
XLA Ops:
  8.1 1.3 copy-done.7
  10.3 49.7 %all-gather.35.cloned.1.call-done = bf16[1,2048,512]{2,1,0:T(8,128)(2,1)} async-done(((bf16[1,2048,128]{2,1,0:T(8,128)(2,1)}), bf16[1,2048,512]{2,1,0:T(8,128)(2,1)}) %all-gather.35.cloned.1.call-update) | async-done | bytes 2097168 | tf_op jit(solution)/shard_map/all_gather | solution.py:17
  60.0 6.5 fusion.6
  68.5 28.6 %reduce-scatter.13.cloned.1.call-done = f32[1024,256]{1,0:T(8,128)} async-done(((f32[1024,512]{1,0:T(8,128)}), f32[1024,256]{1,0:T(8,128)}) %reduce-scatter.13.cloned.1.call-update) | async-done | bytes 1048592 | tf_op jit(solution)/shard_map/reduce_scatter | solution.py:25
  97.1 2.1 convert_element_type.51
  99.3 17.9 %all-gather.37.cloned.1.call-done = bf16[1,3072,512]{2,1,0:T(8,128)(2,1)} async-done(((bf16[1,384,512]{2,1,0:T(8,128)(2,1)}), bf16[1,3072,512]{2,1,0:T(8,128)(2,1)}) %all-gather.37.cloned.1.call-update) | async-done | bytes 3145744 | tf_op jit(solution)/shard_map/all_gather | solution.py:41
  117.1 10.8 %fusion.18 = f32[1536,512]{1,0:T(8,128)} fusion(bf16[3072,1536]{1,0:T(8,128)(2,1)} %param.17, bf16[1,3072,512]{2,1,0:T(8,128)(2,1)} %all-gather.37.cloned.1.call-done), kind=kOutput, calls=%fused_computation.18 | convolution fusion | flops 4831838208 | bytes 15728640 | tf_op jit(solution)/shard_map/dot_general | solution.py:45
  128.0 12.3 %all-gather.15.cloned.1.call-done = bf16[1024,512]{1,0:T(8,128)(2,1)} async-done(((bf16[1024,256]{1,0:T(8,128)(2,1)}), bf16[1024,512]{1,0:T(8,128)(2,1)}) %all-gather.15.cloned.1.call-update) | async-done | bytes 1048592 | tf_op jit(solution)/shard_map/all_gather | solution.py:21
  140.3 3.9 fusion.25
  144.2 44.3 %reduce-scatter.21.cloned.1.call-done = f32[1536,128]{1,0:T(8,128)} async-done(((f32[1536,512]{1,0:T(8,128)}), f32[1536,128]{1,0:T(8,128)}) %reduce-scatter.21.cloned.1.call-update) | async-done | bytes 786448 | tf_op jit(solution)/shard_map/reduce_scatter | solution.py:29
  188.5 1.9 convert_element_type.61
  190.5 43.7 %reduce-scatter.15.cloned.1.call-done = f32[1024,128]{0,1:T(8,128)} async-done(((f32[1024,512]{0,1:T(8,128)}), f32[1024,128]{0,1:T(8,128)}) %reduce-scatter.15.cloned.1.call-update) | async-done | bytes 524304 | tf_op jit(solution)/shard_map/reduce_scatter | solution.py:29
  234.2 1.9 neg.3
  237.0 5.2 gather_fusion
  243.2 13.4 %all-gather.17.cloned.1.call-done = f32[2048,128]{0,1:T(8,128)} async-done(((f32[1024,128]{0,1:T(8,128)}), f32[2048,128]{0,1:T(8,128)}) %all-gather.17.cloned.1.call-update) | async-done | bytes 1048592 | tf_op jit(solution)/shard_map/all_gather | solution.py:118
  256.6 2.4 copy.48
  259.5 1.3 copy.49
  260.9 12.3 %scatter_custom_fusion = f32[2048,128]{1,0:T(8,128)S(1)} fusion(s32[2048]{0:T(1024)S(1)} %bitcast.213, f32[2048,128]{1,0:T(8,128)} %copy.49, f32[]{:T(128)} %constant.180.clone.1), kind=kCustom, calls=%fused_computation.50 | custom fusion | flops 262144 | bytes 1049088 | tf_op jit(solution)/shard_map/scatter-add | solution.py:69
  273.1 1.3 copy.51
  274.4 2.5 copy.50
  277.0 12.1 %scatter_custom_fusion.1 = f32[2048,128]{1,0:T(8,128)S(1)} fusion(s32[2048]{0:T(1024)S(1)} %bitcast.212, f32[2048,128]{1,0:T(8,128)} %copy.50, f32[]{:T(128)} %constant.180.clone.1), kind=kCustom, calls=%fused_computation.48 | custom fusion | flops 262144 | bytes 1049088 | tf_op jit(solution)/shard_map/scatter-add | solution.py:69
  289.1 1.3 copy.52
  290.4 1.7 add.457
  293.1 3.9 fusion.40
  297.0 32.9 %all-gather.19.cloned.1.call-done = bf16[1536,512]{0,1:T(8,128)(2,1)} async-done(((bf16[1536,128]{0,1:T(8,128)(2,1)}), bf16[1536,512]{0,1:T(8,128)(2,1)}) %all-gather.19.cloned.1.call-update) | async-done | bytes 1572880 | tf_op jit(solution)/shard_map/all_gather | solution.py:17
  330.0 7.1 fusion.9
  337.1 2.3 copy.56
  339.4 17.7 %reduce-scatter.23.cloned.1.call-done = f32[768,256]{0,1:T(8,128)} async-done(((f32[768,512]{0,1:T(8,128)}), f32[768,256]{0,1:T(8,128)}) %reduce-scatter.23.cloned.1.call-update) | async-done | bytes 786448 | tf_op jit(solution)/shard_map/reduce_scatter | solution.py:25
  357.1 1.4 fusion.45
  358.6 15.3 %all_gather.52 = bf16[768,512]{0,1:T(8,128)(2,1)} all-gather(bf16[768,256]{0,1:T(8,128)(2,1)S(1)} %fusion.45), channel_id=1, replica_groups=mesh['sec'=4,'row'=2,'col'=4] {'row'}, dimensions={1}, use_global_device_ids=true | all-gather | bytes 1179648 | tf_op jit(solution)/shard_map/all_gather | solution.py:21
  373.9 2.6 collective-permute-done.3
  376.5 7.6 fusion.12
  384.2 21.1 %reduce-scatter.17.cloned.1.call-done = f32[1536,256]{0,1:T(8,128)} async-done(((f32[1536,512]{0,1:T(8,128)}), f32[1536,256]{0,1:T(8,128)}) %reduce-scatter.17.cloned.1.call-update) | async-done | bytes 1572880 | tf_op jit(solution)/shard_map/reduce_scatter | solution.py:25
  405.3 2.1 constant_dynamic-slice_fusion.2
  407.3 60.5 %reduce-scatter.25.cloned.1.call-done = f32[1536,128]{0,1:T(8,128)} async-done(((f32[1536,512]{0,1:T(8,128)}), f32[1536,128]{0,1:T(8,128)}) %reduce-scatter.25.cloned.1.call-update) | async-done | bytes 786448 | tf_op jit(solution)/shard_map/reduce_scatter | solution.py:29
  467.9 1.2 convert_element_type.63
  470.0 2.5 fusion.50
  472.5 16.5 %all_gather.46 = bf16[768,512]{0,1:T(8,128)(2,1)S(1)} all-gather(bf16[768,256]{0,1:T(8,128)(2,1)S(1)} %get-tuple-element.32), channel_id=1, replica_groups=mesh['sec'=4,'row'=2,'col'=4] {'row'}, dimensions={1}, use_global_device_ids=true | all-gather | bytes 1179648 | tf_op jit(solution)/shard_map/all_gather | solution.py:21
  489.0 2.3 convolution_bitcast_fusion
  491.4 3.6 all-gather.29.cloned.1.call-done
  495.2 2.6 collective-permute-done.4
  497.8 3.4 maximum_select_fusion
  501.2 4.1 copy.58
  505.3 4.7 gather_fusion.1
  510.9 1.7 broadcast_select_fusion.1
  512.7 28.3 %reduce-scatter.19.cloned.1.call-done = f32[1024,128]{0,1:T(8,128)} async-done(((f32[1024,512]{0,1:T(8,128)}), f32[1024,128]{0,1:T(8,128)}) %reduce-scatter.19.cloned.1.call-update) | async-done | bytes 524304 | tf_op jit(solution)/shard_map/reduce_scatter | solution.py:29
  542.1 1.5 collective-permute-done.2
  543.6 1.7 fusion.52
  545.3 25.0 %all-gather.31.cloned.1.call-done = bf16[1024,512]{0,1:T(8,128)(2,1)} async-done(((bf16[1024,128]{0,1:T(8,128)(2,1)}), bf16[1024,512]{0,1:T(8,128)(2,1)}) %all-gather.31.cloned.1.call-update) | async-done | bytes 1048592 | tf_op jit(solution)/shard_map/all_gather | solution.py:17
  570.4 3.8 fusion.28
  575.0 20.7 %all-gather.21.cloned.1.call-done = bf16[4096,128]{0,1:T(8,128)(2,1)} async-done(((bf16[512,128]{0,1:T(8,128)(2,1)}), bf16[4096,128]{0,1:T(8,128)(2,1)}) %all-gather.21.cloned.1.call-update) | async-done | bytes 1048592 | tf_op jit(solution)/shard_map/all_gather | solution.py:131
  595.7 1.5 copy.54
  597.2 22.7 %scatter_fusion = f32[1536,128]{1,0:T(8,128)S(1)} fusion(f32[1536,128]{1,0:T(8,128)S(1)} %copy-done.2, s32[4096]{0:T(1024)S(1)} %bitcast.205, f32[4096,128]{1,0:T(8,128)S(1)} %copy.54), kind=kCustom, calls=%fused_computation.4 | custom fusion | flops 524288 | bytes 6307840 | tf_op jit(solution)/shard_map/scatter-add | solution.py:69
  621.6 8.3 %reduce-scatter.27.cloned.1.call-done = f32[1024,256]{0,1:T(8,128)} async-done(((f32[1024,512]{0,1:T(8,128)}), f32[1024,256]{0,1:T(8,128)}) %reduce-scatter.27.cloned.1.call-update) | async-done | bytes 1048592 | tf_op jit(solution)/shard_map/reduce_scatter | solution.py:25
  629.9 2.1 fusion.43
  632.1 37.5 %all-gather.23.cloned.1.call-done = bf16[1536,512]{1,0:T(8,128)(2,1)} async-done(((bf16[1536,128]{1,0:T(8,128)(2,1)}), bf16[1536,512]{1,0:T(8,128)(2,1)}) %all-gather.23.cloned.1.call-update) | async-done | bytes 1572880 | tf_op jit(solution)/shard_map/all_gather | solution.py:17
  669.6 8.2 %fusion.8 = bf16[3072,512]{0,1:T(8,128)(2,1)S(1)} fusion(bf16[1536,512]{1,0:T(8,128)(2,1)} %all-gather.23.cloned.1.call-done, bf16[3072,1536]{1,0:T(8,128)(2,1)} %param.17), kind=kOutput, calls=%fused_computation.14 | convolution fusion | flops 4833411072 | bytes 14155776 | tf_op jit(solution)/shard_map/dot_general | solution.py:45
  677.8 2.8 copy.64
  680.7 10.6 %all-gather.33.cloned.1.call-done = bf16[1024,512]{0,1:T(8,128)(2,1)} async-done(((bf16[1024,256]{0,1:T(8,128)(2,1)}), bf16[1024,512]{0,1:T(8,128)(2,1)}) %all-gather.33.cloned.1.call-update) | async-done | bytes 1048592 | tf_op jit(solution)/shard_map/all_gather | solution.py:21
  691.2 6.9 fusion.15
  701.6 23.3 %reduce-scatter.31.cloned.1.call-done = bf16[384,512]{1,0:T(8,128)(2,1)} async-done(((bf16[3072,512]{1,0:T(8,128)(2,1)}), bf16[384,512]{1,0:T(8,128)(2,1)}) %reduce-scatter.31.cloned.1.call-update) | async-done | bytes 393232
  724.9 1.2 copy.65
  727.3 76.5 %reduce-scatter.29.cloned.1.call-done = f32[2048,128]{0,1:T(8,128)} async-done(((f32[2048,512]{0,1:T(8,128)}), f32[2048,128]{0,1:T(8,128)}) %reduce-scatter.29.cloned.1.call-update) | async-done | bytes 1048592 | tf_op jit(solution)/shard_map/reduce_scatter | solution.py:29
  803.8 2.5 copy.62
  (113 shorter events, 17.1 us)
Async XLA Ops:
  8.0 132.3 %copy-start = (bf16[1,1024,1024]{2,1,0:T(8,128)(2,1)S(1)}, bf16[1,1024,1024]{2,1,0:T(8,128)(2,1)}, u32[]{:S(2)}) copy-start(bf16[1,1024,1024]{2,1,0:T(8,128)(2,1)} %param.14) | copy-start | bytes 6291460
  8.0 1.4 copy-start.7
  8.0 52.0 %all-gather.35.cloned.1.call-start = ((), (), s32[]{:S(2)}) async-start(), calls=%async_computation.29 | async-start | bytes 2621440 | tf_op jit(solution)/shard_map/all_gather | solution.py:17
  10.3 86.9 %reduce-scatter.13.cloned.1.call-start = ((), (), s32[]{:S(2)}) async-start(), calls=%async_computation.10 | async-start | bytes 3145728 | tf_op jit(solution)/shard_map/reduce_scatter | solution.py:25
  66.5 1.1 copy-start.10
  66.5 50.6 %all-gather.37.cloned.1.call-start = ((), (), s32[]{:S(2)}) async-start(), calls=%async_computation.30 | async-start | bytes 3538944 | tf_op jit(solution)/shard_map/all_gather | solution.py:41
  68.5 71.8 %all-gather.15.cloned.1.call-start = ((), (), s32[]{:S(2)}) async-start(), calls=%async_computation.11 | async-start | bytes 1572864 | tf_op jit(solution)/shard_map/all_gather | solution.py:21
  99.2 89.3 %reduce-scatter.21.cloned.1.call-start = ((), (), s32[]{:S(2)}) async-start(), calls=%async_computation.19 | async-start | bytes 3932160 | tf_op jit(solution)/shard_map/reduce_scatter | solution.py:29
  127.9 106.3 %reduce-scatter.15.cloned.1.call-start = ((), (), s32[]{:S(2)}) async-start(), calls=%async_computation.12 | async-start | bytes 2621440 | tf_op jit(solution)/shard_map/reduce_scatter | solution.py:29
  144.2 92.9 %all-gather.25.cloned.1.call-start = ((), (), s32[]{:S(2)}) async-start(), calls=%async_computation.20 | async-start | bytes 3538944 | tf_op jit(solution)/shard_map/all_gather | solution.py:41
  190.4 66.2 %all-gather.17.cloned.1.call-start = ((), (), s32[]{:S(2)}) async-start(), calls=%async_computation.13 | async-start | bytes 1572864 | tf_op jit(solution)/shard_map/all_gather | solution.py:118
  236.1 57.0 %all-gather.27.cloned.1.call-start = ((), (), s32[]{:S(2)}) async-start(), calls=%async_computation.21 | async-start | bytes 1310720 | tf_op jit(solution)/shard_map/all_gather | solution.py:17
  237.0 22.0 %copy-start.11 = (s32[4,2048]{1,0:T(4,128)S(1)}, s32[4,2048]{1,0:T(4,128)}, u32[]{:S(2)}) copy-start(s32[4,2048]{1,0:T(4,128)} %param.18) | copy-start | bytes 98308
  243.1 86.8 %all-gather.19.cloned.1.call-start = ((), (), s32[]{:S(2)}) async-start(), calls=%async_computation.14 | async-start | bytes 1966080 | tf_op jit(solution)/shard_map/all_gather | solution.py:17
  256.6 2.9 copy-start.9
  256.6 17.8 %collective-permute-start = (f32[2048,128]{0,1:T(8,128)}, f32[2048,128]{0,1:T(8,128)}, u32[]{:S(2)}, u32[]{:S(2)}) collective-permute-start(f32[2048,128]{0,1:T(8,128)} %all-gather.17.cloned.1.call-done), channel_id=1, source_target_pairs={{0,8},{8,0},{16,24},{24,16},{1,9},{9,1},{17,25},{25,17},{2,10},{10... | collective-permute-start | bytes 3145736 | tf_op jit(solution)/shard_map/ppermute | solution.py:13
  290.4 1.8 copy-start.5
  293.0 64.1 %reduce-scatter.23.cloned.1.call-start = ((), (), s32[]{:S(2)}) async-start(), calls=%async_computation.22 | async-start | bytes 2359296 | tf_op jit(solution)/shard_map/reduce_scatter | solution.py:25
  297.0 108.3 %reduce-scatter.17.cloned.1.call-start = ((), (), s32[]{:S(2)}) async-start(), calls=%async_computation.15 | async-start | bytes 4718592 | tf_op jit(solution)/shard_map/reduce_scatter | solution.py:25
  337.1 130.8 %reduce-scatter.25.cloned.1.call-start = ((), (), s32[]{:S(2)}) async-start(), calls=%async_computation.23 | async-start | bytes 3932160 | tf_op jit(solution)/shard_map/reduce_scatter | solution.py:29
  373.9 2.6 collective-permute-start.3
  384.1 23.2 %copy-start.6 = (bf16[1024,128]{0,1:T(8,128)(2,1)S(1)}, bf16[1024,128]{0,1:T(8,128)(2,1)}, u32[]{:S(2)}) copy-start(bf16[1024,128]{0,1:T(8,128)(2,1)} %broadcast_select_fusion) | copy-start | bytes 786436
  384.1 110.8 %all-gather.29.cloned.1.call-start = ((), (), s32[]{:S(2)}) async-start(), calls=%async_computation.24 | async-start | bytes 1572864 | tf_op jit(solution)/shard_map/all_gather | solution.py:153
  407.3 62.7 %collective-permute-start.1 = (f32[768,256]{0,1:T(8,128)}, f32[768,256]{0,1:T(8,128)}, u32[]{:S(2)}, u32[]{:S(2)}) collective-permute-start(f32[768,256]{0,1:T(8,128)} %constant_dynamic-slice_fusion.2), channel_id=1, source_target_pairs={{0,8},{8,0},{16,24},{24,16},{1,9},{9,1},{17,25},{25,17},{2,10},{10... | collective-permute-start | bytes 2359304 | tf_op jit(solution)/shard_map/ppermute | solution.py:13
  469.9 71.1 %reduce-scatter.19.cloned.1.call-start = ((), (), s32[]{:S(2)}) async-start(), calls=%async_computation.16 | async-start | bytes 2621440 | tf_op jit(solution)/shard_map/reduce_scatter | solution.py:29
  470.0 19.0 %copy-start.14 = (bf16[1,1024,768]{2,1,0:T(8,128)(2,1)S(1)}, bf16[1,1024,768]{2,1,0:T(8,128)(2,1)}, u32[]{:S(2)}) copy-start(bf16[1,1024,768]{2,1,0:T(8,128)(2,1)} %param.16) | copy-start | bytes 4718596
  491.3 3.7 copy-start.12
  491.3 79.0 %all-gather.31.cloned.1.call-start = ((), (), s32[]{:S(2)}) async-start(), calls=%async_computation.25 | async-start | bytes 1310720 | tf_op jit(solution)/shard_map/all_gather | solution.py:17
  494.9 2.9 collective-permute-start.4
  512.6 83.0 %all-gather.21.cloned.1.call-start = ((), (), s32[]{:S(2)}) async-start(), calls=%async_computation.17 | async-start | bytes 1179648 | tf_op jit(solution)/shard_map/all_gather | solution.py:131
  542.0 1.6 collective-permute-start.2
  545.3 84.6 %reduce-scatter.27.cloned.1.call-start = ((), (), s32[]{:S(2)}) async-start(), calls=%async_computation.26 | async-start | bytes 3145728 | tf_op jit(solution)/shard_map/reduce_scatter | solution.py:25
  574.2 0.7 copy-start.13
  574.2 23.0 %copy-start.2 = (f32[1536,128]{1,0:T(8,128)S(1)}, f32[1536,128]{1,0:T(8,128)}, u32[]{:S(2)}) copy-start(f32[1536,128]{1,0:T(8,128)} %param.22) | copy-start | bytes 2359300
  574.2 95.4 %all-gather.23.cloned.1.call-start = ((), (), s32[]{:S(2)}) async-start(), calls=%async_computation.18 | async-start | bytes 1966080 | tf_op jit(solution)/shard_map/all_gather | solution.py:17
  619.9 1.4 copy-start.8
  620.7 70.6 %all-gather.33.cloned.1.call-start = ((), (), s32[]{:S(2)}) async-start(), calls=%async_computation.27 | async-start | bytes 1572864 | tf_op jit(solution)/shard_map/all_gather | solution.py:21
  632.0 92.8 %reduce-scatter.31.cloned.1.call-start = ((), (), s32[]{:S(2)}) async-start(), calls=%async_computation.31 | async-start | bytes 3538944
  680.6 123.2 %reduce-scatter.29.cloned.1.call-start = ((), (), s32[]{:S(2)}) async-start(), calls=%async_computation.28 | async-start | bytes 5242880 | tf_op jit(solution)/shard_map/reduce_scatter | solution.py:29
  698.2 1.1 copy-start.4
  698.2 2.3 copy-start.3
  726.1 80.2 %copy-start.1 = (bf16[1,1024,1024]{2,1,0:T(8,128)(2,1)S(1)}, bf16[1,1024,1024]{2,1,0:T(8,128)(2,1)}, u32[]{:S(2)}) copy-start(bf16[1,1024,1024]{2,1,0:T(8,128)(2,1)} %param.14) | copy-start | bytes 6291460
Sparse Core Ops, SparseCore 0:
  11.0 48.9 all-gather.34
  66.7 30.4 reduce-scatter.12
  128.1 60.3 reduce-scatter.20
  190.6 43.5 reduce-scatter.14
  470.0 24.8 all-gather.28
  497.1 43.8 reduce-scatter.18
  543.1 27.1 all-gather.30
  572.8 22.8 all-gather.20
  597.9 31.8 reduce-scatter.26
  631.9 37.6 all-gather.22
  671.7 19.4 all-gather.32
Sparse Core Ops, SparseCore 1:
  69.5 47.6 all-gather.36
  119.1 21.1 all-gather.14
  190.5 31.9 all-gather.24
  236.2 20.4 all-gather.16
  258.8 27.9 all-gather.26
  293.1 36.8 all-gather.18
  332.1 25.0 reduce-scatter.22
  359.2 46.0 reduce-scatter.16
  407.4 60.4 reduce-scatter.24
  680.7 44.1 reduce-scatter.30
  727.0 76.7 reduce-scatter.28
where the time goes:
time: 815 us; the launch traced here: 814 us
  waiting for transfers between devices  583 us (72%)
  other arithmetic  75.1 us (9%)
  matrix products  61 us (7%)
  local copies, waits for them, and re-layouts  45.6 us (6%)
  blocking collectives  31.8 us (4%)
  between operations  16.1 us (2%)
    reduce_scatter x5, waiting for transfers between devices, sum_cols(): return lax.psum_scatter(block, 'col', scatter_dimension=1, tiled=True)  253 us
    all_gather x5, waiting for transfers between devices, spread_cols(): return lax.all_gather(block, 'col', axis=1, tiled=True)  145 us
    reduce_scatter x4, waiting for transfers between devices, sum_rows(): return lax.psum_scatter(block, 'row', scatter_dimension=1, tiled=True)  75.6 us
    dot_general x10, matrix products, matmul(): return jnp.dot(left, right, preferred_element_type=jnp.float32)  61 us
    scatter-add x3, other arithmetic, place_rows(): jnp.zeros((count, values.shape[1]), jnp.float32).at[target]  47 us
    all_gather x2, blocking collectives, spread_rows(): return lax.all_gather(block, 'row', axis=1, tiled=True)  31.8 us
    unnamed x23, waiting for transfers between devices  23.6 us
    all_gather x2, waiting for transfers between devices, spread_rows(): return lax.all_gather(block, 'row', axis=1, tiled=True)  22.8 us
  transfers between devices with their start and end apart: 27, of which 23 were waited for; matrix products, arithmetic and copies ran while one was open for 21% of the time, Pallas kernels for 0%

commit v1 on v0

--- a/solution.py
+++ b/solution.py
@@ -18,7 +18,11 @@
 
 
 def spread_rows(block):
-    return lax.all_gather(block, "row", axis=1, tiled=True)
+    enter_state = lambda local_array: jnp.concatenate(
+        lax.all_to_all(jnp.stack([local_array for _ in range(lax.axis_size("row"))]), "row", 0, 0),
+        axis=1,
+    )
+    return enter_state(block)
 
 
 def sum_rows(block):

time: 815 us -> 842 us (1.033)
  blocking collectives: 31.8 us -> 66.7 us
  waiting for transfers between devices: 583 us -> 572 us
    all_to_all x0 -> x4, blocking collectives: none -> 66.7 us  [spread_rows(): lax.all_to_all(jnp.stack([local_array for _ in range(lax.axis_size('row')...]
    all_gather x2, waiting for transfers between devices: 17.9 us -> 57.1 us  [root_gather(): return lax.all_gather(block, ('sec', 'row'), axis=0, tiled=True)]
    all_gather x2 -> x0, blocking collectives: 31.8 us -> none  [spread_rows(): return lax.all_gather(block, 'row', axis=1, tiled=True)]
    all_gather x5, waiting for transfers between devices: 145 us -> 119 us  [spread_cols(): return lax.all_gather(block, 'col', axis=1, tiled=True)]
    all_gather x2 -> x0, waiting for transfers between devices: 22.8 us -> none  [spread_rows(): return lax.all_gather(block, 'row', axis=1, tiled=True)]
    all_gather x1, waiting for transfers between devices: 3.57 us -> 19.2 us  [per_device(): side_rows = lax.all_gather(front_x, 'row', axis=0, tiled=True)]
    all_gather x1, waiting for transfers between devices: 20.7 us -> 8.81 us  [per_device(): lax.all_gather(contrib_two.astype(jnp.bfloat16), ('sec', 'row'), axis=0,...]
    reduce_scatter x5, waiting for transfers between devices: 253 us -> 243 us  [sum_cols(): return lax.psum_scatter(block, 'col', scatter_dimension=1, tiled=True)]
  transfers between devices with their start and end apart: 27 -> 25, of which waited for: 23 -> 22; matrix products, arithmetic and copies ran while one was open for 21% -> 22% of each run, Pallas kernels for 0% -> 0%
where the time goes in v1:
time: 842 us; the launch traced here: 840 us
  waiting for transfers between devices  572 us (68%)
  other arithmetic  76.6 us (9%)
  blocking collectives  66.7 us (8%)
  matrix products  59.8 us (7%)
  local copies, waits for them, and re-layouts  50 us (6%)
  between operations  14.7 us (2%)
    reduce_scatter x5, waiting for transfers between devices, sum_cols(): return lax.psum_scatter(block, 'col', scatter_dimension=1, tiled=True)  243 us
    all_gather x5, waiting for transfers between devices, spread_cols(): return lax.all_gather(block, 'col', axis=1, tiled=True)  119 us
    reduce_scatter x4, waiting for transfers between devices, sum_rows(): return lax.psum_scatter(block, 'row', scatter_dimension=1, tiled=True)  76.7 us
    all_to_all x4, blocking collectives, spread_rows(): lax.all_to_all(jnp.stack([local_array for _ in range(lax.axis_size('row')...  66.7 us
    dot_general x10, matrix products, matmul(): return jnp.dot(left, right, preferred_element_type=jnp.float32)  59.8 us
    all_gather x2, waiting for transfers between devices, root_gather(): return lax.all_gather(block, ('sec', 'row'), axis=0, tiled=True)  57.1 us
    scatter-add x3, other arithmetic, place_rows(): jnp.zeros((count, values.shape[1]), jnp.float32).at[target]  47.5 us
    unnamed x21, waiting for transfers between devices  24.1 us
  transfers between devices with their start and end apart: 25, of which 22 were waited for; matrix products, arithmetic and copies ran while one was open for 22% of the time, Pallas kernels for 0%

profile of v1, /device:TPU:0, one launch (start us, length us, event | category | flops | bytes accessed | tf_op | source)
XLA Modules:
  0.0 840.5 jit_solution(15535686813954171231)
XLA Ops:
  7.2 1.3 copy-done.5
  9.5 1.9 convert_element_type.59
  11.5 47.7 %all-gather.29.cloned.1.call-done = bf16[1,2048,512]{2,1,0:T(8,128)(2,1)} async-done(((bf16[1,2048,128]{2,1,0:T(8,128)(2,1)}), bf16[1,2048,512]{2,1,0:T(8,128)(2,1)}) %all-gather.29.cloned.1.call-update) | async-done | bytes 2097168 | tf_op jit(solution)/shard_map/all_gather | solution.py:17
  59.1 6.6 fusion.6
  65.8 26.2 %all-gather.31.cloned.1.call-done = bf16[1,3072,512]{2,1,0:T(8,128)(2,1)} async-done(((bf16[1,384,512]{2,1,0:T(8,128)(2,1)}), bf16[1,3072,512]{2,1,0:T(8,128)(2,1)}) %all-gather.31.cloned.1.call-update) | async-done | bytes 3145744 | tf_op jit(solution)/shard_map/all_gather | solution.py:45
  92.0 10.7 %fusion.18 = f32[1536,512]{1,0:T(8,128)} fusion(bf16[3072,1536]{1,0:T(8,128)(2,1)} %param.17, bf16[1,3072,512]{2,1,0:T(8,128)(2,1)} %all-gather.31.cloned.1.call-done), kind=kOutput, calls=%fused_computation.18 | convolution fusion | flops 4831838208 | bytes 15728640 | tf_op jit(solution)/shard_map/dot_general | solution.py:49
  102.8 23.9 %reduce-scatter.13.cloned.1.call-done = f32[1024,256]{1,0:T(8,128)} async-done(((f32[1024,512]{1,0:T(8,128)}), f32[1024,256]{1,0:T(8,128)}) %reduce-scatter.13.cloned.1.call-update) | async-done | bytes 1048592 | tf_op jit(solution)/shard_map/reduce_scatter | solution.py:29
  128.1 16.1 %all_to_all.20 = bf16[2,1024,256]{2,1,0:T(8,128)(2,1)S(1)} all-to-all(bf16[2,1024,256]{2,1,0:T(8,128)(2,1)S(1)} %pad_maximum_fusion), channel_id=1, replica_groups=mesh['sec'=4,'row'=2,'col'=4] {'row'}, dimensions={0} | all-to-all | bytes 2097152 | tf_op jit(solution)/shard_map/all_to_all | solution.py:22
  145.6 3.8 fusion.25
  149.5 40.4 %reduce-scatter.21.cloned.1.call-done = f32[1536,128]{1,0:T(8,128)} async-done(((f32[1536,512]{1,0:T(8,128)}), f32[1536,128]{1,0:T(8,128)}) %reduce-scatter.21.cloned.1.call-update) | async-done | bytes 786448 | tf_op jit(solution)/shard_map/reduce_scatter | solution.py:33
  189.9 1.9 convert_element_type.61
  191.9 43.7 %reduce-scatter.15.cloned.1.call-done = f32[1024,128]{0,1:T(8,128)} async-done(((f32[1024,512]{0,1:T(8,128)}), f32[1024,128]{0,1:T(8,128)}) %reduce-scatter.15.cloned.1.call-update) | async-done | bytes 524304 | tf_op jit(solution)/shard_map/reduce_scatter | solution.py:33
  235.6 1.9 neg.3
  238.4 30.9 %all-gather.21.cloned.1.call-done = bf16[12288,128]{1,0:T(8,128)(2,1)} async-done(((bf16[1536,128]{1,0:T(8,128)(2,1)}), bf16[12288,128]{1,0:T(8,128)(2,1)}) %all-gather.21.cloned.1.call-update) | async-done | bytes 3145744 | tf_op jit(solution)/shard_map/all_gather | solution.py:45
  269.4 5.2 gather_fusion
  275.5 17.3 %all-gather.13.cloned.1.call-done = f32[2048,128]{0,1:T(8,128)} async-done(((f32[1024,128]{0,1:T(8,128)}), f32[2048,128]{0,1:T(8,128)}) %all-gather.13.cloned.1.call-update) | async-done | bytes 1048592 | tf_op jit(solution)/shard_map/all_gather | solution.py:122
  292.8 2.4 copy.51
  295.7 1.3 copy.53
  297.0 12.3 %scatter_custom_fusion = f32[2048,128]{1,0:T(8,128)S(1)} fusion(s32[2048]{0:T(1024)S(1)} %bitcast.240, f32[2048,128]{1,0:T(8,128)} %copy.53, f32[]{:T(128)} %constant.180.clone.1), kind=kCustom, calls=%fused_computation.56 | custom fusion | flops 262144 | bytes 1049088 | tf_op jit(solution)/shard_map/scatter-add | solution.py:73
  309.3 1.3 copy.55
  310.6 2.5 copy.54
  313.2 12.1 %scatter_custom_fusion.1 = f32[2048,128]{1,0:T(8,128)S(1)} fusion(s32[2048]{0:T(1024)S(1)} %bitcast.239, f32[2048,128]{1,0:T(8,128)} %copy.54, f32[]{:T(128)} %constant.180.clone.1), kind=kCustom, calls=%fused_computation.54 | custom fusion | flops 262144 | bytes 1049088 | tf_op jit(solution)/shard_map/scatter-add | solution.py:73
  325.3 1.3 copy.56
  326.6 1.7 add.457
  329.3 3.9 fusion.40
  333.2 33.2 %all-gather.15.cloned.1.call-done = bf16[1536,512]{0,1:T(8,128)(2,1)} async-done(((bf16[1536,128]{0,1:T(8,128)(2,1)}), bf16[1536,512]{0,1:T(8,128)(2,1)}) %all-gather.15.cloned.1.call-update) | async-done | bytes 1572880 | tf_op jit(solution)/shard_map/all_gather | solution.py:17
  366.4 7.1 fusion.9
  373.6 2.3 copy.60
  375.9 17.7 %reduce-scatter.23.cloned.1.call-done = f32[768,256]{0,1:T(8,128)} async-done(((f32[768,512]{0,1:T(8,128)}), f32[768,256]{0,1:T(8,128)}) %reduce-scatter.23.cloned.1.call-update) | async-done | bytes 786448 | tf_op jit(solution)/shard_map/reduce_scatter | solution.py:29
  393.6 1.4 fusion.51
  395.1 20.6 %all_to_all.21 = bf16[2,768,256]{1,2,0:T(8,128)(2,1)} all-to-all(bf16[2,768,256]{1,2,0:T(8,128)(2,1)S(1)} %pad_maximum_fusion.3), channel_id=1, replica_groups=mesh['sec'=4,'row'=2,'col'=4] {'row'}, dimensions={0} | all-to-all | bytes 1572864 | tf_op jit(solution)/shard_map/all_to_all | solution.py:22
  415.7 2.6 collective-permute-done.3
  418.4 7.7 fusion.12
  426.2 18.4 %reduce-scatter.17.cloned.1.call-done = f32[1536,256]{0,1:T(8,128)} async-done(((f32[1536,512]{0,1:T(8,128)}), f32[1536,256]{0,1:T(8,128)}) %reduce-scatter.17.cloned.1.call-update) | async-done | bytes 1572880 | tf_op jit(solution)/shard_map/reduce_scatter | solution.py:29
  444.6 2.1 constant_dynamic-slice_fusion.2
  446.6 2.6 collective-permute-done.1
  449.3 2.3 convert_bitcast_fusion.1
  451.7 13.8 %all_to_all.22 = bf16[2,768,256]{1,2,0:T(8,128)(2,1)S(1)} all-to-all(bf16[2,768,256]{1,2,0:T(8,128)(2,1)S(1)} %pad_maximum_fusion.2), channel_id=1, replica_groups=mesh['sec'=4,'row'=2,'col'=4] {'row'}, dimensions={0} | all-to-all | bytes 1572864 | tf_op jit(solution)/shard_map/all_to_all | solution.py:22
  465.5 2.4 convolution_bitcast_fusion
  468.8 38.4 %reduce-scatter.25.cloned.1.call-done = f32[1536,128]{0,1:T(8,128)} async-done(((f32[1536,512]{0,1:T(8,128)}), f32[1536,128]{0,1:T(8,128)}) %reduce-scatter.25.cloned.1.call-update) | async-done | bytes 786448 | tf_op jit(solution)/shard_map/reduce_scatter | solution.py:33
  509.3 43.7 %reduce-scatter.19.cloned.1.call-done = f32[1024,128]{0,1:T(8,128)} async-done(((f32[1024,512]{0,1:T(8,128)}), f32[1024,128]{0,1:T(8,128)}) %reduce-scatter.19.cloned.1.call-update) | async-done | bytes 524304 | tf_op jit(solution)/shard_map/reduce_scatter | solution.py:33
  553.0 1.7 constant_dynamic-slice_fusion.1
  556.3 19.2 %all-gather.25.cloned.1.call-done = bf16[4096,128]{0,1:T(8,128)(2,1)} async-done(((bf16[2048,128]{0,1:T(8,128)(2,1)}), bf16[4096,128]{0,1:T(8,128)(2,1)}) %all-gather.25.cloned.1.call-update) | async-done | bytes 1048592 | tf_op jit(solution)/shard_map/all_gather | solution.py:157
  575.5 1.7 fusion.53
  578.5 4.0 maximum_select_fusion
  582.5 4.1 copy.62
  586.6 4.8 gather_fusion.1
  592.5 8.8 %all-gather.17.cloned.1.call-done = bf16[4096,128]{0,1:T(8,128)(2,1)} async-done(((bf16[512,128]{0,1:T(8,128)(2,1)}), bf16[4096,128]{0,1:T(8,128)(2,1)}) %all-gather.17.cloned.1.call-update) | async-done | bytes 1048592 | tf_op jit(solution)/shard_map/all_gather | solution.py:135
  601.3 2.6 copy.58
  603.9 23.2 %scatter_fusion = f32[1536,128]{1,0:T(8,128)S(1)} fusion(f32[1536,128]{1,0:T(8,128)S(1)} %copy-done.1, s32[4096]{0:T(1024)S(1)} %bitcast.232, f32[4096,128]{1,0:T(8,128)} %copy.58), kind=kCustom, calls=%fused_computation.4 | custom fusion | flops 524288 | bytes 6307840 | tf_op jit(solution)/shard_map/scatter-add | solution.py:73
  628.0 3.3 all-gather.27.cloned.1.call-done
  631.3 3.9 fusion.28
  635.3 35.1 %all-gather.19.cloned.1.call-done = bf16[1536,512]{1,0:T(8,128)(2,1)} async-done(((bf16[1536,128]{1,0:T(8,128)(2,1)}), bf16[1536,512]{1,0:T(8,128)(2,1)}) %all-gather.19.cloned.1.call-update) | async-done | bytes 1572880 | tf_op jit(solution)/shard_map/all_gather | solution.py:17
  670.4 9.3 %fusion.8 = bf16[3072,512]{0,1:T(8,128)(2,1)} fusion(bf16[1536,512]{1,0:T(8,128)(2,1)} %all-gather.19.cloned.1.call-done, bf16[3072,1536]{1,0:T(8,128)(2,1)} %param.17), kind=kOutput, calls=%fused_computation.14 | convolution fusion | flops 4833411072 | bytes 14155776 | tf_op jit(solution)/shard_map/dot_general | solution.py:49
  679.8 4.7 copy.68
  684.5 1.6 copy.59
  686.1 16.6 %reduce-scatter.27.cloned.1.call-done = f32[1024,256]{0,1:T(8,128)} async-done(((f32[1024,512]{0,1:T(8,128)}), f32[1024,256]{0,1:T(8,128)}) %reduce-scatter.27.cloned.1.call-update) | async-done | bytes 1048592 | tf_op jit(solution)/shard_map/reduce_scatter | solution.py:29
  702.7 1.5 fusion.46
  704.3 16.2 %all_to_all.23 = bf16[2,1024,256]{1,2,0:T(8,128)(2,1)S(1)} all-to-all(bf16[2,1024,256]{1,2,0:T(8,128)(2,1)S(1)} %pad_maximum_fusion.1), channel_id=1, replica_groups=mesh['sec'=4,'row'=2,'col'=4] {'row'}, dimensions={0} | all-to-all | bytes 2097152 | tf_op jit(solution)/shard_map/all_to_all | solution.py:22
  720.4 4.3 fusion.15
  724.8 2.4 copy.64
  728.3 23.8 %reduce-scatter.31.cloned.1.call-done = bf16[384,512]{1,0:T(8,128)(2,1)} async-done(((bf16[3072,512]{1,0:T(8,128)(2,1)}), bf16[384,512]{1,0:T(8,128)(2,1)}) %reduce-scatter.31.cloned.1.call-update) | async-done | bytes 393232
  754.6 76.5 %reduce-scatter.29.cloned.1.call-done = f32[2048,128]{0,1:T(8,128)} async-done(((f32[2048,512]{0,1:T(8,128)}), f32[2048,128]{0,1:T(8,128)}) %reduce-scatter.29.cloned.1.call-update) | async-done | bytes 1048592 | tf_op jit(solution)/shard_map/reduce_scatter | solution.py:33
  831.1 2.5 copy.66
  (106 shorter events, 19.1 us)
Async XLA Ops:
  7.2 138.4 %copy-start = (bf16[1,1024,1024]{2,1,0:T(8,128)(2,1)S(1)}, bf16[1,1024,1024]{2,1,0:T(8,128)(2,1)}, u32[]{:S(2)}) copy-start(bf16[1,1024,1024]{2,1,0:T(8,128)(2,1)} %param.14) | copy-start | bytes 6291460
  7.2 1.4 copy-start.5
  7.2 52.0 %all-gather.29.cloned.1.call-start = ((), (), s32[]{:S(2)}) async-start(), calls=%async_computation.31 | async-start | bytes 2621440 | tf_op jit(solution)/shard_map/all_gather | solution.py:17
  9.4 82.6 %all-gather.31.cloned.1.call-start = ((), (), s32[]{:S(2)}) async-start(), calls=%async_computation.32 | async-start | bytes 3538944 | tf_op jit(solution)/shard_map/all_gather | solution.py:45
  11.4 115.3 %reduce-scatter.13.cloned.1.call-start = ((), (), s32[]{:S(2)}) async-start(), calls=%async_computation.14 | async-start | bytes 3145728 | tf_op jit(solution)/shard_map/reduce_scatter | solution.py:29
  65.8 124.2 %reduce-scatter.21.cloned.1.call-start = ((), (), s32[]{:S(2)}) async-start(), calls=%async_computation.22 | async-start | bytes 3932160 | tf_op jit(solution)/shard_map/reduce_scatter | solution.py:33
  102.8 132.8 %reduce-scatter.15.cloned.1.call-start = ((), (), s32[]{:S(2)}) async-start(), calls=%async_computation.15 | async-start | bytes 2621440 | tf_op jit(solution)/shard_map/reduce_scatter | solution.py:33
  149.5 119.9 %all-gather.21.cloned.1.call-start = ((), (), s32[]{:S(2)}) async-start(), calls=%async_computation.23 | async-start | bytes 3538944 | tf_op jit(solution)/shard_map/all_gather | solution.py:45
  191.9 100.9 %all-gather.13.cloned.1.call-start = ((), (), s32[]{:S(2)}) async-start(), calls=%async_computation.16 | async-start | bytes 1572864 | tf_op jit(solution)/shard_map/all_gather | solution.py:122
  237.5 91.7 %all-gather.23.cloned.1.call-start = ((), (), s32[]{:S(2)}) async-start(), calls=%async_computation.24 | async-start | bytes 1310720 | tf_op jit(solution)/shard_map/all_gather | solution.py:17
  238.4 56.7 %copy-start.7 = (s32[4,2048]{1,0:T(4,128)S(1)}, s32[4,2048]{1,0:T(4,128)}, u32[]{:S(2)}) copy-start(s32[4,2048]{1,0:T(4,128)} %param.18) | copy-start | bytes 98308
  275.4 91.0 %all-gather.15.cloned.1.call-start = ((), (), s32[]{:S(2)}) async-start(), calls=%async_computation.17 | async-start | bytes 1966080 | tf_op jit(solution)/shard_map/all_gather | solution.py:17
  292.8 2.9 copy-start.6
  292.8 17.8 %collective-permute-start = (f32[2048,128]{0,1:T(8,128)}, f32[2048,128]{0,1:T(8,128)}, u32[]{:S(2)}, u32[]{:S(2)}) collective-permute-start(f32[2048,128]{0,1:T(8,128)} %all-gather.13.cloned.1.call-done), channel_id=1, source_target_pairs={{0,8},{8,0},{16,24},{24,16},{1,9},{9,1},{17,25},{25,17},{2,10},{10... | collective-permute-start | bytes 3145736 | tf_op jit(solution)/shard_map/ppermute | solution.py:13
  326.6 1.8 copy-start.3
  329.2 64.4 %reduce-scatter.23.cloned.1.call-start = ((), (), s32[]{:S(2)}) async-start(), calls=%async_computation.25 | async-start | bytes 2359296 | tf_op jit(solution)/shard_map/reduce_scatter | solution.py:29
  333.1 111.4 %reduce-scatter.17.cloned.1.call-start = ((), (), s32[]{:S(2)}) async-start(), calls=%async_computation.18 | async-start | bytes 4718592 | tf_op jit(solution)/shard_map/reduce_scatter | solution.py:29
  373.5 133.6 %reduce-scatter.25.cloned.1.call-start = ((), (), s32[]{:S(2)}) async-start(), calls=%async_computation.26 | async-start | bytes 3932160 | tf_op jit(solution)/shard_map/reduce_scatter | solution.py:33
  415.7 2.6 collective-permute-start.3
  426.1 126.9 %reduce-scatter.19.cloned.1.call-start = ((), (), s32[]{:S(2)}) async-start(), calls=%async_computation.19 | async-start | bytes 2621440 | tf_op jit(solution)/shard_map/reduce_scatter | solution.py:33
  446.6 2.6 collective-permute-start.1
  446.6 18.8 %copy-start.10 = (bf16[1,1024,768]{2,1,0:T(8,128)(2,1)S(1)}, bf16[1,1024,768]{2,1,0:T(8,128)(2,1)}, u32[]{:S(2)}) copy-start(bf16[1,1024,768]{2,1,0:T(8,128)(2,1)} %param.16) | copy-start | bytes 4718596
  467.8 0.9 copy-start.4
  467.9 107.6 %all-gather.25.cloned.1.call-start = ((), (), s32[]{:S(2)}) async-start(), calls=%async_computation.27 | async-start | bytes 1572864 | tf_op jit(solution)/shard_map/all_gather | solution.py:157
  509.2 92.1 %all-gather.17.cloned.1.call-start = ((), (), s32[]{:S(2)}) async-start(), calls=%async_computation.20 | async-start | bytes 1179648 | tf_op jit(solution)/shard_map/all_gather | solution.py:135
  554.7 20.8 %collective-permute-start.2 = (f32[512,128]{0,1:T(8,128)}, f32[512,128]{0,1:T(8,128)S(1)}, u32[]{:S(2)}, u32[]{:S(2)}) collective-permute-start(f32[512,128]{0,1:T(8,128)} %constant_dynamic-slice_fusion.1), channel_id=1, source_target_pairs={{0,8},{8,0},{16,24},{24,16},{1,9},{9,1},{17,25},{25,17},{2,10},{10... | collective-permute-start | bytes 786440 | tf_op jit(solution)/shard_map/ppermute | solution.py:13
  575.5 3.0 collective-permute-start.4
  577.2 54.1 %all-gather.27.cloned.1.call-start = ((), (), s32[]{:S(2)}) async-start(), calls=%async_computation.28 | async-start | bytes 1310720 | tf_op jit(solution)/shard_map/all_gather | solution.py:17
  586.6 5.7 copy-start.8
  591.5 12.4 %copy-start.1 = (f32[1536,128]{1,0:T(8,128)S(1)}, f32[1536,128]{1,0:T(8,128)}, u32[]{:S(2)}) copy-start(f32[1536,128]{1,0:T(8,128)} %param.22) | copy-start | bytes 2359300
  592.3 78.1 %all-gather.19.cloned.1.call-start = ((), (), s32[]{:S(2)}) async-start(), calls=%async_computation.21 | async-start | bytes 1966080 | tf_op jit(solution)/shard_map/all_gather | solution.py:17
  627.9 74.7 %reduce-scatter.27.cloned.1.call-start = ((), (), s32[]{:S(2)}) async-start(), calls=%async_computation.29 | async-start | bytes 3145728 | tf_op jit(solution)/shard_map/reduce_scatter | solution.py:29
  635.2 116.9 %reduce-scatter.31.cloned.1.call-start = ((), (), s32[]{:S(2)}) async-start(), calls=%async_computation.33 | async-start | bytes 3538944
  684.4 146.7 %reduce-scatter.29.cloned.1.call-start = ((), (), s32[]{:S(2)}) async-start(), calls=%async_computation.30 | async-start | bytes 5242880 | tf_op jit(solution)/shard_map/reduce_scatter | solution.py:33
  702.7 17.8 %copy-start.9 = (bf16[1,1024,2048]{2,1,0:T(8,128)(2,1)S(1)}, bf16[1,1024,2048]{2,1,0:T(8,128)(2,1)}, u32[]{:S(2)}) copy-start(bf16[1,1024,2048]{2,1,0:T(8,128)(2,1)} %param.13) | copy-start | bytes 12582916
  724.8 2.4 copy-start.2
Sparse Core Ops, SparseCore 0:
  10.1 48.9 all-gather.28
  61.6 30.3 all-gather.30
  94.8 31.8 reduce-scatter.12
  129.5 60.3 reduce-scatter.20
  192.1 43.5 reduce-scatter.14
  237.9 31.3 all-gather.20
  271.5 21.2 all-gather.12
  294.9 27.9 all-gather.22
  329.3 37.0 all-gather.14
  368.5 25.0 reduce-scatter.22
  395.8 48.6 reduce-scatter.16
  446.7 60.4 reduce-scatter.24
  509.5 43.5 reduce-scatter.18
  555.0 20.4 all-gather.24
  577.8 23.4 all-gather.16
  603.3 27.9 all-gather.26
  633.3 37.0 all-gather.18
  672.5 30.1 reduce-scatter.26
  706.1 46.0 reduce-scatter.30
  754.3 76.7 reduce-scatter.28
